TPU v7x, 256 devices: a whole 4x4x8 slice. The times are simulated.
256 devices in a mesh: ctx: 64 (over z, y_hi, x), head: 4 (over y_lo, core).
Axes of the slice: x: 4, y: 4 (y_hi: 2, y_lo: 2; y = y_hi * 2 + y_lo), z: 8, core: 2. Of those that a mesh axis runs over, the one named last changes fastest.
Arguments:
- queries: bfloat16 [12288, 4096], P('ctx', 'head'), may hold values from -6 to 6
- attention_keys: bfloat16 [12288, 512], P('ctx'), may hold values from -6 to 6
- attention_values: bfloat16 [12288, 512], P('ctx'), may hold values from -6 to 6
- attn_gate: bfloat16 [12288, 4096], P('ctx', 'head'), may hold values from -6 to 6
- segment_ids: int32 [12288], P('ctx'), may hold values from 0 to 7, never falling along the last dimension, each value on 1 to 3072 neighbouring positions
- value_proj: bfloat16 [4096, 4096], P(None, 'head'), may hold values from -0.09375 to 0.09375
- linear_queries: bfloat16 [12288, 2048], P('ctx', 'head'), may hold values from -6 to 6
- linear_keys: bfloat16 [12288, 2048], P('ctx', 'head'), may hold values from -6 to 6
- conv_queries: bfloat16 [4, 2048], P(None, 'head'), may hold values from -3 to 3
- conv_keys: bfloat16 [4, 2048], P(None, 'head'), may hold values from -3 to 3
- conv_values: bfloat16 [4, 4096], P(None, 'head'), may hold values from -3 to 3
- decay_logits: float32 [12288, 32], P('ctx', 'head'), may hold values from -16 to 0
- beta_logits: float32 [12288, 32], P('ctx', 'head'), may hold values from -16 to 2
- decay_base: float32 [32], P('head'), may hold values from -0.5 to 0.5
- decay_bias: float32 [32], P('head'), may hold values from -0.5 to 0.5
- output_gate: bfloat16 [12288, 4096], P('ctx', 'head'), may hold values from -6 to 6
- output_gain: float32 [128], replicated, may hold values from 0.1 to 1.9
- rezero_gate: float32 [4096], P('head'), may hold values from 0.5 to 1.5
Outputs:
- layer_output: bfloat16 [12288, 4096], P('ctx', 'head')
Inputs may be any that keep to these rules, and one draw needn't show every extreme that they name: `segment_ids`: each document spans at most 3072 consecutive tokens, and one spans exactly that many.
All inputs are finite; a program needn't handle non-finite values.
Results may differ from a plain program's by a relative error of at most 0.017.
Values may be sent and summed in bfloat16 or wider, within the bound.
A program may use at most 192 MiB of HBM per device.

v0:
```python
import functools

import jax
import jax.numpy as jnp
from jax import lax
from jax.experimental import pallas as pl
from jax.experimental.pallas import tpu as pltpu
from jax.sharding import PartitionSpec as P

MESH = pl.DeviceIdType.MESH
EPSILON = 1e-06
NEGATIVE = -1e30
HIGH = lax.Precision.HIGHEST
F32 = jnp.float32
BF16 = jnp.bfloat16

ROWS = 192
HALF = 96
WINDOW = 17
HEADS = 8


def coords():
    ctx = lax.axis_index("ctx")
    head = lax.axis_index("head")
    z, place = lax.div(ctx, 8), lax.rem(ctx, 8)
    y_hi, x = lax.div(place, 4), lax.rem(place, 4)
    y_lo, core = lax.div(head, 2), lax.rem(head, 2)
    return ctx, head, z, place, y_hi, x, y_lo, core


def greet(sources):
    barrier = pltpu.get_barrier_semaphore()
    for device in sources:
        pl.semaphore_signal(barrier, inc=1, device_id=device, device_id_type=MESH)
    pl.semaphore_wait(barrier, len(sources))


def push(src, dst, send_sem, recv_sem, device):
    return pltpu.make_async_remote_copy(
        src_ref=src,
        dst_ref=dst,
        send_sem=send_sem,
        recv_sem=recv_sem,
        device_id=device,
        device_id_type=MESH,
    )


def window_sources():
    ctx, head, z, place, y_hi, x, y_lo, core = coords()
    partner = (ctx, y_lo * 2 + 1 - core)
    across = (z * 8 + (1 - y_hi) * 4 + x, (1 - y_lo) * 2 + core)
    below = (lax.rem(z + 7, 8) * 8 + place, head)
    beside = [(z * 8 + y_hi * 4 + lax.rem(x + d, 4), head) for d in (1, 3, 2)]
    return [partner, across, below] + beside


def window_steps(
    keys, values, seg, kv, segs, own, own_seg, load_sem, y_s, y_r, z_s, z_r, x_s, x_r, f_s, f_r
):
    ctx, head, z, place, y_hi, x, y_lo, core = coords()
    partner = (ctx, y_lo * 2 + 1 - core)
    across = (z * 8 + (1 - y_hi) * 4 + x, (1 - y_lo) * 2 + core)
    above = (lax.rem(z + 1, 8) * 8 + place, head)
    beside = [(z * 8 + y_hi * 4 + lax.rem(x + d, 4), head) for d in (1, 3, 2)]
    rows = pl.ds(pl.multiple_of(core * HALF, 16), HALF)
    mine = pl.ds(pl.multiple_of(y_lo * 256, 256), 256)
    other = pl.ds(pl.multiple_of((1 - y_lo) * 256, 256), 256)

    local = [
        pltpu.make_async_copy(keys.at[:, mine], own.at[0, :, pl.ds(0, 256)], load_sem.at[0]),
        pltpu.make_async_copy(values.at[:, mine], own.at[0, :, pl.ds(256, 256)], load_sem.at[1]),
        pltpu.make_async_copy(keys.at[rows, other], own.at[1, rows, pl.ds(0, 256)], load_sem.at[2]),
        pltpu.make_async_copy(
            values.at[rows, other], own.at[1, rows, pl.ds(256, 256)], load_sem.at[3]
        ),
        pltpu.make_async_copy(seg, own_seg, load_sem.at[4]),
    ]
    for copy in local:
        copy.start()
    yield
    for copy in local:
        copy.wait()
    keep = [
        pltpu.make_async_copy(own.at[0], kv.at[0, y_hi, x], load_sem.at[5]),
        pltpu.make_async_copy(own_seg, segs.at[x, 0, y_hi], load_sem.at[6]),
    ]
    for copy in keep:
        copy.start()

    y_copy = [
        push(own.at[1, rows], kv.at[0, y_hi, x, rows], y_s.at[0], y_r.at[0], across),
        push(own_seg, segs.at[x, 0, y_hi], y_s.at[1], y_r.at[1], across),
    ]
    for copy in y_copy:
        copy.start()
    y_back = [
        push(own.at[1, rows], kv.at[0, 1 - y_hi, x, rows], y_s.at[0], y_r.at[0], across),
        push(own_seg, segs.at[x, 0, 1 - y_hi], y_s.at[1], y_r.at[1], across),
    ]

    def z_push(step, yh, index):
        return push(
            kv.at[step, yh, x, rows], kv.at[step + 1, yh, x, rows], z_s.at[index], z_r.at[index], above
        )

    def forward(step, yh, xs, index):
        return push(
            kv.at[step, yh, xs, rows], kv.at[step, yh, xs, rows], f_s.at[index], f_r.at[index], partner
        )

    def forwarded(step, yh, xs, index):
        back = pl.ds(pl.multiple_of((1 - core) * HALF, 16), HALF)
        return push(
            kv.at[step, yh, xs, back], kv.at[step, yh, xs, back], f_s.at[index], f_r.at[index], partner
        )

    z_first = push(own.at[0, rows], kv.at[1, y_hi, x, rows], z_s.at[0], z_r.at[0], above)
    z_first.start()

    def x_push(k, step, yh, index, src=None):
        source = kv.at[step, yh, x, rows] if src is None else src
        return push(source, kv.at[step, yh, x, rows], x_s.at[k, index], x_r.at[k, index], beside[k])

    def later(k, yh):
        dest = y_hi * 4 + lax.rem(x + (1, 3, 2)[k], 4)
        return yh * 4 + x < dest

    for k in range(3):
        early = later(k, y_hi)

        @pl.when(early)
        def _(k=k):
            x_push(k, 0, y_hi, 0, own.at[0, rows]).start()

    yield
    for copy in y_back:
        copy.wait_recv()
    z_second = z_push(0, 1 - y_hi, 1)
    z_second.start()
    z_seg = push(segs.at[x, 0], segs.at[x, 1], z_s.at[4], z_r.at[4], above)
    keep[1].wait()
    z_seg.start()
    for k in range(3):
        early = later(k, 1 - y_hi)

        @pl.when(early)
        def _(k=k):
            x_push(k, 0, 1 - y_hi, 1).start()

    forwards = [(0, 1 - y_hi, x)]
    forward(*forwards[0], 0).start()

    yield
    for yh, index in ((y_hi, 0), (1 - y_hi, 1)):
        z_push(0, yh, index).wait_recv()
        z_push(1, yh, 2 + index).start()
        for k in range(3):
            x_push(k, 1, yh, 2 + index).start()
        forward(1, yh, x, len(forwards)).start()
        forwards.append((1, yh, x))
    yield
    z_seg.wait_recv()
    z_seg_on = push(segs.at[x, 1], segs.at[x, 2], z_s.at[5], z_r.at[5], above)
    z_seg_on.start()
    for yh, index in ((y_hi, 0), (1 - y_hi, 1)):
        z_push(1, yh, 2 + index).wait_recv()
        for k in range(3):
            late = jnp.logical_not(later(k, yh))

            @pl.when(late)
            def _(k=k, yh=yh, index=index):
                x_push(k, 2, yh, index).start()

        forward(2, yh, x, len(forwards)).start()
        forwards.append((2, yh, x))
    yield
    z_seg_on.wait_recv()
    x_seg = [
        push(segs.at[x], segs.at[x], x_s.at[k, 4], x_r.at[k, 4], beside[k]) for k in range(3)
    ]
    for copy in x_seg:
        copy.start()

    def came(k, step, yh, index):
        xs = lax.rem(x + (3, 1, 2)[k], 4)
        return push(
            kv.at[step, yh, xs, rows], kv.at[step, yh, xs, rows], x_s.at[k, index], x_r.at[k, index], beside[k]
        )

    def choice(k, yh):
        xs = lax.rem(x + (3, 1, 2)[k], 4)
        return jnp.where(yh * 4 + xs < place, 0, 2)

    yield
    for k in range(3):
        xs = lax.rem(x + (3, 1, 2)[k], 4)
        for yh, index in ((y_hi, 0), (1 - y_hi, 1)):
            came(k, 1, yh, 2 + index).wait_recv()
            forward(1, yh, xs, len(forwards)).start()
            forwards.append((1, yh, xs))
    yield
    for k in range(3):
        xs = lax.rem(x + (3, 1, 2)[k], 4)
        for yh, index in ((y_hi, 0), (1 - y_hi, 1)):
            step = choice(k, yh)
            came(k, step, yh, index).wait_recv()
            forward(step, yh, xs, len(forwards)).start()
            forwards.append((step, yh, xs))
        x_seg_in = push(segs.at[xs], segs.at[xs], x_s.at[k, 4], x_r.at[k, 4], beside[k])
        x_seg_in.wait_recv()
    yield
    for index, where in enumerate(forwards):
        forwarded(*where, index).wait_recv()
    keep[0].wait()
    for copy in y_copy:
        copy.wait_send()
    z_first.wait_send()
    z_second.wait_send()
    z_seg.wait_send()
    z_seg_on.wait_send()
    for index in (2, 3):
        z_push(1, y_hi, index).wait_send()
    for k in range(3):
        for index in range(4):
            x_push(k, 1, y_hi, index).wait_send()
        x_seg[k].wait_send()
    for index, where in enumerate(forwards):
        forward(*where, index).wait_send()


def attention_kernel(slots, kv, segs, seg_query, queries, gate, out, q_all, first, m_sc, l_sc, acc):
    step = pl.program_id(0)
    lanes = 4 * ROWS

    @pl.when(step == 0)
    def _():
        for h in range(4):
            q_all[h * ROWS : (h + 1) * ROWS, :] = (
                queries[:, h * 256 : (h + 1) * 256].astype(F32) * 0.0625
            ).astype(BF16)
        m_sc[...] = jnp.full(m_sc.shape, NEGATIVE, F32)
        l_sc[...] = jnp.zeros(l_sc.shape, F32)
        acc[...] = jnp.zeros(acc.shape, F32)
        begin = jnp.zeros((1, lanes), jnp.int32)
        missing = slots[2 * WINDOW]
        for doc in range(8):
            less = jnp.zeros((8, 128), jnp.int32)
            for b in range(WINDOW):
                block = segs[slots[WINDOW + b]]
                less = less + jnp.where((block < doc) & (b >= missing), 1, 0)
            total = jnp.sum(less) + missing * ROWS
            begin = jnp.where(seg_query[...] == doc, total, begin)
        first[...] = jnp.broadcast_to(begin, first.shape)

    block = lax.rem(WINDOW - 1 + step, WINDOW)
    keys, values = kv[0, :, 0:256], kv[0, :, 256:512]
    scores = lax.dot_general(
        keys, q_all[...], (((1,), (1,)), ((), ())), preferred_element_type=F32
    )
    key_pos = block * ROWS + lax.broadcasted_iota(jnp.int32, (ROWS, lanes), 0)
    token = lax.broadcasted_iota(jnp.int32, (1, lanes), 1)
    for h in range(1, 4):
        token = jnp.where(token >= ROWS, token - ROWS, token)
    last = (WINDOW - 1) * ROWS + token
    allowed = (key_pos >= first[0:1, :]) & (key_pos <= last)
    scores = jnp.where(allowed, scores, NEGATIVE)
    m_old = m_sc[0:1, :]
    m_new = jnp.maximum(m_old, jnp.max(scores, axis=0, keepdims=True))
    scale = jnp.exp(m_old - m_new)
    weights = jnp.exp(scores - m_new)
    l_sc[0:1, :] = l_sc[0:1, :] * scale + jnp.sum(weights, axis=0, keepdims=True)
    m_sc[0:1, :] = m_new
    added = lax.dot_general(
        values, weights.astype(BF16), (((0,), (0,)), ((), ())), preferred_element_type=F32
    )
    acc[...] = acc[...] * scale + added

    @pl.when(step == WINDOW - 1)
    def _():
        mean = jnp.transpose(acc[...] / l_sc[0:1, :])
        for h in range(4):
            g = gate[:, h * 256 : (h + 1) * 256].astype(F32)
            out[:, h * 256 : (h + 1) * 256] = (
                jax.nn.sigmoid(g) * mean[h * ROWS : (h + 1) * ROWS, :]
            ).astype(BF16)


def attention(slots, kv, segs, seg_query, queries, gate):
    full = lambda shape: pl.BlockSpec(shape, lambda s, slots: (0,) * len(shape))
    lanes = 4 * ROWS
    return pl.pallas_call(
        attention_kernel,
        out_shape=jax.ShapeDtypeStruct((ROWS, 1024), BF16),
        grid_spec=pltpu.PrefetchScalarGridSpec(
            num_scalar_prefetch=1,
            grid=(WINDOW,),
            in_specs=[
                pl.BlockSpec(
                    (1, ROWS, 512),
                    lambda s, slots: (slots[lax.rem(WINDOW - 1 + s, WINDOW)], 0, 0),
                ),
                full((24, 8, 128)),
                full((1, lanes)),
                full((ROWS, 1024)),
                full((ROWS, 1024)),
            ],
            out_specs=full((ROWS, 1024)),
            scratch_shapes=[
                pltpu.VMEM((lanes, 256), BF16),
                pltpu.VMEM((8, lanes), jnp.int32),
                pltpu.VMEM((8, lanes), F32),
                pltpu.VMEM((8, lanes), F32),
                pltpu.VMEM((256, lanes), F32),
            ],
        ),
        name="window_attention",
    )(slots, kv, segs, seg_query, queries, gate)


PIECES = 3


def heads_kernel(own, out, l_sem, p_s, p_r, a_s, a_r, f_s, f_r):
    ctx, head, z, place, y_hi, x, y_lo, core = coords()
    partner = (ctx, y_lo * 2 + 1 - core)
    across = (ctx, (1 - y_lo) * 2 + core)
    greet([partner, across])
    size = ROWS // PIECES

    def part(i, h):
        return out.at[pl.ds(i * size, size), pl.ds(pl.multiple_of(h * 1024, 1024), 1024)]

    def piece(i):
        return own.at[pl.ds(i * size, size)]

    far, farther = (1 - y_lo) * 2 + core, (1 - y_lo) * 2 + 1 - core
    keep = [pltpu.make_async_copy(piece(i), part(i, head), l_sem.at[i]) for i in range(PIECES)]
    for i in range(PIECES):
        push(piece(i), part(i, head), a_s.at[i], a_r.at[i], across).start()
        push(piece(i), part(i, head), p_s.at[i], p_r.at[i], partner).start()
        keep[i].start()
    for i in range(PIECES):
        push(piece(i), part(i, far), a_s.at[i], a_r.at[i], across).wait_recv()
        push(part(i, far), part(i, far), f_s.at[i], f_r.at[i], partner).start()
    for i in range(PIECES):
        near = y_lo * 2 + 1 - core
        push(piece(i), part(i, near), p_s.at[i], p_r.at[i], partner).wait()
        push(part(i, far), part(i, farther), f_s.at[i], f_r.at[i], partner).wait()
        push(piece(i), part(i, far), a_s.at[i], a_r.at[i], across).wait_send()
        keep[i].wait()


def all_heads(own):
    dma = pltpu.SemaphoreType.DMA
    return pl.pallas_call(
        heads_kernel,
        out_shape=jax.ShapeDtypeStruct((ROWS, 4096), BF16),
        in_specs=[pl.BlockSpec(memory_space=pltpu.VMEM)],
        out_specs=pl.BlockSpec(memory_space=pl.ANY),
        scratch_shapes=[dma((PIECES,))] * 7,
        compiler_params=pltpu.CompilerParams(collective_id=1, has_side_effects=True),
        name="all_heads",
    )(own)


def mm(a, b, precision=None):
    return jnp.dot(a, b, precision=precision, preferred_element_type=F32)


def mm_t(a, b, precision=None):
    return lax.dot_general(
        a, b, (((1,), (1,)), ((), ())), precision=precision, preferred_element_type=F32
    )


def split(x):
    high = x.astype(BF16)
    return high, (x - high.astype(F32)).astype(BF16)


def mm_split(a, b, product=mm):
    (ah, al), (bh, bl) = a, b
    return product(ah, bh) + (product(ah, bl) + product(al, bh))


def mm_low(a, b):
    return mm(a.astype(BF16), b.astype(BF16))


def causal(ext, taps, width):
    total = jnp.zeros((ROWS, width), F32)
    for m in range(4):
        total = total + taps[m : m + 1, :] * ext[13 + m : 13 + m + ROWS, 0:width]
    return total / (1.0 + jnp.exp(-total))


def triangle(size, strict):
    row = lax.broadcasted_iota(jnp.int32, (size, size), 0)
    col = lax.broadcasted_iota(jnp.int32, (size, size), 1)
    return (col < row) if strict else (col <= row)


def inverse_lower(systems):
    row = lax.broadcasted_iota(jnp.int32, (ROWS, ROWS), 0)
    col = lax.broadcasted_iota(jnp.int32, (ROWS, ROWS), 1)
    unit = jnp.where(row == col, 1.0, 0.0)
    block = lax.div(row, 8) == lax.div(col, 8)
    powers = [jnp.where(block, -m, 0.0) for m in systems]
    inverses = [unit + p for p in powers]
    for _ in range(2):
        powers = [mm_low(p, p) for p in powers]
        inverses = [x + mm_low(x, p) for x, p in zip(inverses, powers)]
    size = 8
    while size < ROWS:
        pair = 2 * size
        below = (lax.div(row, pair) == lax.div(col, pair)) & (lax.div(row, size) != lax.div(col, size))
        if pair >= ROWS:
            below = lax.div(row, size) != lax.div(col, size)
        lows = [x.astype(BF16) for x in inverses]
        inner = [
            mm(jnp.where(below, m, 0.0).astype(BF16), x) for m, x in zip(systems, lows)
        ]
        inverses = [
            x - mm(low, i.astype(BF16)) for x, low, i in zip(inverses, lows, inner)
        ]
        size = pair
        yield None
    splits = [split(x) for x in inverses]
    rests = [
        (unit - x) - mm_split(split(m), xs) for m, x, xs in zip(systems, inverses, splits)
    ]
    yield [x + mm(xs[0], r.astype(BF16)) for x, xs, r in zip(inverses, splits, rests)]


def linear_kernel(
    lq, lk, cq, ck, decay, beta, keys, values, seg,
    h_out, eff_out, g_out, px_out, mz_out, kv, segs,
    own, own_seg, w_load, wy_s, wy_r, wz_s, wz_r, wx_s, wx_r, wf_s, wf_r,
    halo, ext, q_sc, k_sc, t_own, t_all, row_sc, p_own, p_all,
    hs, hr, ts, tr, zs, zr,
):
    ctx, head, z, place, y_hi, x, y_lo, core = coords()
    following = (lax.rem(ctx + 1, 64), head)
    previous = (lax.rem(ctx + 63, 64), head)
    plane = [(z * 8 + lax.rem(place + d, 8), head) for d in range(1, 8)]
    column = [(lax.rem(z + d, 8) * 8 + place, head) for d in range(1, 8)]
    transfers = window_steps(
        keys, values, seg, kv, segs, own, own_seg, w_load,
        wy_s, wy_r, wz_s, wz_r, wx_s, wx_r, wf_s, wf_r,
    )
    next(transfers)
    greet([previous] + plane + column + window_sources())
    tail = pl.ds(ROWS - 16, 16)
    edge = [
        push(lq.at[tail], halo.at[0], hs.at[0], hr.at[0], following),
        push(lk.at[tail], halo.at[1], hs.at[1], hr.at[1], following),
    ]
    for copy in edge:
        copy.start()
    next(transfers)
    for copy in edge:
        copy.wait()
    begins = ctx == 0
    for source, taps, index, target in ((lq, cq, 0, q_sc), (lk, ck, 1, k_sc)):
        ext[0:16, :] = jnp.where(begins, 0.0, halo[index].astype(F32))
        ext[16 : 16 + ROWS, :] = source[...].astype(F32)
        conv = causal(ext, taps, 512)
        for n in range(4):
            part = conv[:, n * 128 : (n + 1) * 128]
            part = part / jnp.sqrt(jnp.sum(part * part, axis=1, keepdims=True) + EPSILON)
            if index == 0:
                part = part * (1.0 / 128.0**0.5)
            target[n] = part
        next(transfers)
    lower = triangle(ROWS, False)
    strict = triangle(ROWS, True)
    ones = jnp.where(lower, 1.0, 0.0)
    row = lax.broadcasted_iota(jnp.int32, (ROWS, ROWS), 0)
    col = lax.broadcasted_iota(jnp.int32, (ROWS, ROWS), 1)
    unit = jnp.where(row == col, 1.0, 0.0)
    unit_k = jnp.where(
        lax.broadcasted_iota(jnp.int32, (128, 128), 0)
        == lax.broadcasted_iota(jnp.int32, (128, 128), 1),
        1.0,
        0.0,
    )
    sum_row = mm_t(decay[...], ones, HIGH)
    sum_col = mm_t(ones, decay[...], HIGH)
    beta_col = mm_t(unit, beta[...], HIGH)
    group = 2
    for base in range(0, HEADS, group):
        parts, systems = [], []
        for e in range(base, base + group):
            q, k = q_sc[e // 2], k_sc[e // 2]
            if e % 2 == 0:
                k_split = split(k)
                key_key = mm_split(k_split, k_split, mm_t)
                query_key = mm_split(split(q), k_split, mm_t)
            c_col, c_row = sum_col[:, e : e + 1], sum_row[e : e + 1, :]
            b_col, b_row = beta_col[:, e : e + 1], beta[e : e + 1, :]
            fade = jnp.exp(jnp.where(lower, c_col - c_row, NEGATIVE))
            systems.append(jnp.where(strict, b_col * key_key * fade, 0.0))
            parts.append((q, k, c_col, b_col, b_row, query_key * fade))
        for inverses in inverse_lower(systems):
            pass
        for e, inverse, (q, k, c_col, b_col, b_row, scores) in zip(
            range(base, base + group), inverses, parts
        ):
            grown = jnp.exp(c_col)
            inverse = split(inverse)
            scores = split(scores)
            weight_keys = split(mm_split(inverse, split((b_col * grown) * k)))
            eff_out[e] = (grown * q - mm_split(scores, weight_keys)).astype(BF16)
            h_out[e] = (mm_split(scores, inverse) * b_row).astype(BF16)
            final = c_col[ROWS - 1 : ROWS, :]
            decayed = split(jnp.transpose(jnp.exp(final - c_col) * k))
            t_own[e] = (jnp.exp(final) * unit_k - mm_split(decayed, weight_keys)).astype(BF16)
            g_out[e] = (mm_split(decayed, inverse) * b_row).astype(BF16)
        next(transfers, None)

    sends = []
    for d in range(1, 8):
        owner = lax.rem(place + d, 8)
        copy = push(t_own.at[owner], t_all.at[8 - d], ts.at[d - 1], tr.at[7 - d], plane[d - 1])
        copy.start()
        sends.append(copy)
    t_all[0] = t_own[place]
    for d in range(1, 8):
        push(t_own.at[0], t_all.at[8 - d], ts.at[d - 1], tr.at[7 - d], plane[d - 1]).wait_recv()
    row_sc[...] = jnp.zeros(row_sc.shape, F32)
    row_sc[:, 0:128] = unit_k
    px_out[0] = row_sc[...].astype(BF16)
    for i in range(8):
        current = t_all[lax.rem(i - place + 8, 8)]
        width = (i + 1) * 128
        high, low = split(row_sc[:, 0:width])
        row_sc[:, 0:width] = mm(current, high) + mm(current, low)
        row_sc[:, width : width + 128] = unit_k
        px_out[i + 1] = row_sc[...].astype(BF16)
    p_own[...] = row_sc[:, 0:128].astype(BF16)
    for d in range(1, 8):
        copy = push(p_own, p_all.at[d - 1], zs.at[d - 1], zr.at[d - 1], column[d - 1])
        copy.start()
        sends.append(copy)
    for d in range(1, 8):
        push(p_own, p_all.at[d - 1], zs.at[d - 1], zr.at[d - 1], column[d - 1]).wait_recv()
    running = unit_k
    for r in range(1, 8):
        valid = z >= r
        mz_out[:, (r - 1) * 128 : r * 128] = jnp.where(valid, running, 0.0).astype(BF16)
        if r < 7:
            high, low = split(running)
            running = mm(high, p_all[r - 1]) + mm(low, p_all[r - 1])
    for copy in sends:
        copy.wait_send()
    for _ in transfers:
        pass


def linear(lq, lk, cq, ck, decay, beta, keys, values, seg_tile):
    dma = pltpu.SemaphoreType.DMA
    vmem = pl.BlockSpec(memory_space=pltpu.VMEM)
    anywhere = pl.BlockSpec(memory_space=pl.ANY)
    return pl.pallas_call(
        linear_kernel,
        out_shape=(
            jax.ShapeDtypeStruct((HEADS, ROWS, ROWS), BF16),
            jax.ShapeDtypeStruct((HEADS, ROWS, 128), BF16),
            jax.ShapeDtypeStruct((HEADS, 128, ROWS), BF16),
            jax.ShapeDtypeStruct((9, 128, 1152), BF16),
            jax.ShapeDtypeStruct((128, 896), BF16),
            jax.ShapeDtypeStruct((3, 2, 4, ROWS, 512), BF16),
            jax.ShapeDtypeStruct((4, 3, 2, 8, 128), jnp.int32),
        ),
        in_specs=[vmem] * 6 + [anywhere] * 3,
        out_specs=[vmem] * 5 + [anywhere] * 2,
        scratch_shapes=[
            pltpu.VMEM((2, ROWS, 512), BF16),
            pltpu.VMEM((8, 128), jnp.int32),
            dma((7,)),
            dma((2,)),
            dma((2,)),
            dma((6,)),
            dma((6,)),
            dma((3, 5)),
            dma((3, 5)),
            dma((17,)),
            dma((17,)),
            pltpu.VMEM((2, 16, 512), BF16),
            pltpu.VMEM((16 + ROWS, 512), F32),
            pltpu.VMEM((4, ROWS, 128), F32),
            pltpu.VMEM((4, ROWS, 128), F32),
            pltpu.VMEM((8, 128, 128), BF16),
            pltpu.VMEM((8, 128, 128), BF16),
            pltpu.VMEM((128, 1152), F32),
            pltpu.VMEM((128, 128), BF16),
            pltpu.VMEM((7, 128, 128), BF16),
            dma((2,)),
            dma((2,)),
            dma((7,)),
            dma((7,)),
            dma((7,)),
            dma((7,)),
        ],
        compiler_params=pltpu.CompilerParams(collective_id=2, has_side_effects=True),
        name="linear_operators",
    )(lq, lk, cq, ck, decay, beta, keys, values, seg_tile)


def delta_kernel(
    value_in, cv, h_in, eff_in, g_in, px_in, mz_in, attn, gate, gain, rezero, out,
    halo, ext, v_sc, b_own, b_all, local, l_own, l_all, within, s_own, s_all,
    hs, hr, bs, br, zs, zr, ss, sr,
):
    ctx, head, z, place, y_hi, x, y_lo, core = coords()
    following = (lax.rem(ctx + 1, 64), head)
    previous = (lax.rem(ctx + 63, 64), head)
    plane = [(z * 8 + lax.rem(place + d, 8), head) for d in range(1, 8)]
    column = [(lax.rem(z + d, 8) * 8 + place, head) for d in range(1, 8)]
    greet([previous] + plane + column)
    edge = push(value_in.at[pl.ds(ROWS - 16, 16)], halo, hs.at[0], hr.at[0], following)
    edge.start()
    ext[16 : 16 + ROWS, :] = value_in[...].astype(F32)
    edge.wait()
    ext[0:16, :] = jnp.where(ctx == 0, 0.0, halo[...].astype(F32))
    v_sc[...] = causal(ext, cv, 1024).astype(BF16)
    for e in range(HEADS):
        b_own[e] = mm(g_in[e], v_sc[:, e * 128 : (e + 1) * 128]).astype(BF16)
    sends = []
    for d in range(1, 8):
        owner = lax.rem(place + d, 8)
        copy = push(b_own.at[owner], b_all.at[place], bs.at[d - 1], br.at[d - 1], plane[d - 1])
        copy.start()
        sends.append(copy)
    b_all[place] = b_own[place]
    for e in range(HEADS):
        local[e] = mm(h_in[e], v_sc[:, e * 128 : (e + 1) * 128])
    for d in range(1, 8):
        source = lax.rem(place + 8 - d, 8)
        push(b_own.at[0], b_all.at[source], bs.at[d - 1], br.at[d - 1], plane[d - 1]).wait_recv()
    blocks = b_all[...].reshape(8 * 128, 128)
    l_own[...] = mm(px_in[8, :, 128:1152], blocks).astype(BF16)
    for d in range(1, 8):
        copy = push(l_own, l_all.at[d - 1], zs.at[d - 1], zr.at[d - 1], column[d - 1])
        copy.start()
        sends.append(copy)
    for i in range(8):
        within[i] = mm(px_in[i, :, 128:1152], blocks)
    for d in range(1, 8):
        push(l_own, l_all.at[d - 1], zs.at[d - 1], zr.at[d - 1], column[d - 1]).wait_recv()
    entry = mm(mz_in[...], l_all[...].reshape(7 * 128, 128)).astype(BF16)
    for i in range(8):
        s_own[i] = (mm(px_in[i, :, 0:128], entry) + within[i]).astype(BF16)
    for d in range(1, 8):
        target = lax.rem(place + d, 8)
        copy = push(s_own.at[target], s_all.at[place], ss.at[d - 1], sr.at[d - 1], plane[d - 1])
        copy.start()
        sends.append(copy)
    s_all[place] = s_own[place]
    for d in range(1, 8):
        source = lax.rem(place + 8 - d, 8)
        push(s_own.at[0], s_all.at[source], ss.at[d - 1], sr.at[d - 1], plane[d - 1]).wait_recv()
    for e in range(HEADS):
        cols = slice(e * 128, (e + 1) * 128)
        delta = local[e] + mm(eff_in[e], s_all[e])
        norm = delta / jnp.sqrt(jnp.mean(delta * delta, axis=1, keepdims=True) + EPSILON)
        g = gate[:, cols].astype(F32)
        gated = norm * gain[...] * (g * jax.nn.sigmoid(g))
        out[:, cols] = (attn[:, cols].astype(F32) + rezero[:, cols] * gated).astype(BF16)
    for copy in sends:
        copy.wait_send()


def delta(value_in, cv, ops, attn, gate, gain, rezero):
    dma = pltpu.SemaphoreType.DMA
    vmem = pl.BlockSpec(memory_space=pltpu.VMEM)
    return pl.pallas_call(
        delta_kernel,
        out_shape=jax.ShapeDtypeStruct((ROWS, 1024), BF16),
        in_specs=[vmem] * 11,
        out_specs=vmem,
        scratch_shapes=[
            pltpu.VMEM((16, 1024), BF16),
            pltpu.VMEM((16 + ROWS, 1024), F32),
            pltpu.VMEM((ROWS, 1024), BF16),
            pltpu.VMEM((8, 128, 128), BF16),
            pltpu.VMEM((8, 128, 128), BF16),
            pltpu.VMEM((8, ROWS, 128), F32),
            pltpu.VMEM((128, 128), BF16),
            pltpu.VMEM((7, 128, 128), BF16),
            pltpu.VMEM((8, 128, 128), F32),
            pltpu.VMEM((8, 128, 128), BF16),
            pltpu.VMEM((8, 128, 128), BF16),
            dma((1,)),
            dma((1,)),
            dma((7,)),
            dma((7,)),
            dma((7,)),
            dma((7,)),
            dma((7,)),
            dma((7,)),
        ],
        compiler_params=pltpu.CompilerParams(collective_id=3, has_side_effects=True),
        name="delta_rule",
    )(value_in, cv, *ops, attn, gate, gain, rezero)


def body(
    queries,
    attention_keys,
    attention_values,
    attn_gate,
    segment_ids,
    value_proj,
    linear_queries,
    linear_keys,
    conv_queries,
    conv_keys,
    conv_values,
    decay_logits,
    beta_logits,
    decay_base,
    decay_bias,
    output_gate,
    output_gain,
    rezero_gate,
):
    ctx = lax.axis_index("ctx")
    seg_tile = jnp.pad(segment_ids, (0, 1024 - ROWS), constant_values=127).reshape(8, 128)
    log_decay = -jnp.exp(decay_base)[:, None] * jax.nn.softplus(
        decay_logits.T + decay_bias[:, None]
    )
    beta = jax.nn.sigmoid(beta_logits.T)
    *ops, kv, segs = linear(
        linear_queries,
        linear_keys,
        conv_queries.astype(F32),
        conv_keys.astype(F32),
        log_decay,
        beta,
        attention_keys,
        attention_values,
        seg_tile,
    )
    back = 16 - jnp.arange(WINDOW, dtype=jnp.int32)
    source = ctx - back + 64
    step = source // 8
    step = (ctx + 64) // 8 - step
    y_hi, x = (source // 4) % 2, source % 4
    missing = jnp.maximum(16 - ctx, 0).astype(jnp.int32).reshape(1)
    slots = jnp.concatenate(
        [step * 8 + y_hi * 4 + x, x * 6 + step * 2 + y_hi, missing]
    ).astype(jnp.int32)
    seg_query = jnp.tile(segment_ids, 4).reshape(1, 4 * ROWS)
    attn_out = attention(
        slots, kv.reshape(24, ROWS, 512), segs.reshape(24, 8, 128), seg_query, queries, attn_gate
    )
    everything = all_heads(attn_out)
    squares = jnp.mean(jnp.square(everything.astype(F32)), axis=1, keepdims=True)
    summed = jnp.dot(everything, value_proj, preferred_element_type=F32)
    value_in = (summed / jnp.sqrt(squares + EPSILON)).astype(BF16)
    return delta(
        value_in,
        conv_values.astype(F32),
        ops,
        attn_out,
        output_gate,
        output_gain.reshape(1, 128),
        rezero_gate.reshape(1, 1024),
    )


def solution(mesh):
    placed = (
        P("ctx", "head"),
        P("ctx", None),
        P("ctx", None),
        P("ctx", "head"),
        P("ctx"),
        P(None, "head"),
        P("ctx", "head"),
        P("ctx", "head"),
        P(None, "head"),
        P(None, "head"),
        P(None, "head"),
        P("ctx", "head"),
        P("ctx", "head"),
        P("head"),
        P("head"),
        P("ctx", "head"),
        P(),
        P("head"),
    )
    return jax.shard_map(
        body, mesh=mesh, in_specs=placed, out_specs=P("ctx", "head"), check_vma=False
    )
```

profile of v0, /device:TPU:8, one launch (start us, length us, event | category | flops | bytes accessed | tf_op | source)
XLA Modules:
  0.0 139.6 jit_solution(7911798890053562451)
XLA Ops:
  0.0 0.7 pad_add_fusion.slots
  0.7 0.7 exponential_negate_fusion
  1.3 1.4 fusion.1.decay
  2.7 1.3 convert_element_type.15.cq
  4.0 1.3 convert_element_type.16.ck
  5.3 1.3 divide_bitcast_fusion.beta
  6.6 1.3 pad_bitcast_fusion.seg
  7.9 53.9 %linear_operators.1 = (bf16[8,192,192]{2,1,0:T(8,128)(2,1)}, bf16[8,192,128]{2,1,0:T(8,128)(2,1)}, bf16[8,128,192]{2,1,0:T(8,128)(2,1)}, bf16[9,128,1152]{2,1,0:...) custom-call(bf16[192,512]{1,0:T(8,128)(2,1)} %lq.1, ...), custom_call_target="tpu_custom_call" | custom-call | tf_op jit(solution)/shard_map/linear_operators/pallas_call | solution.py:566
  61.7 0.7 tile.2
  62.4 0.7 reshape_tile.3.seg_query
  63.1 17.0 %window_attention.1.own.attn = bf16[192,1024]{1,0:T(8,128)(2,1)} custom-call(s32[35]{0:T(128)} %pad_add_fusion.slots, bf16[24,192,512]{2,1,0:T(8,128)(2,1)} %bitcast.27, s32[24,8,128]{2,1,0:T(8,128)} %bitcast.28, s32[1,768]{1,0:T(1,128)} %reshape_tile.3.seg_query, bf16[192,1024]{1,0:T(8,128)(2,1)} %queries.1, bf16[192,1024]{1,0:T(8,128)(2,1)} %gate.2), custom_call_target="tpu_custom_call" | custom-call | tf_op jit(solution)/shard_map/window_attention/pallas_call | solution.py:293
  80.1 14.4 %all_heads.1 = bf16[192,4096]{1,0:T(8,128)(2,1)} custom-call(bf16[192,1024]{1,0:T(8,128)(2,1)} %window_attention.1.own.attn), custom_call_target="tpu_custom_call" | custom-call | tf_op jit(solution)/shard_map/all_heads/pallas_call | solution.py:357
  94.5 1.8 %multiply_reduce_fusion = f32[192]{0:T(256)S(1)} fusion(bf16[192,4096]{1,0:T(8,128)(2,1)} %all_heads.1), kind=kLoop, calls=%fused_computation | loop fusion | flops 2359104 | bytes 1573632 | tf_op jit(solution)/shard_map/reduce_sum | solution.py:761
  96.3 0.0 copy-start
  96.3 6.4 %fusion.value_in = bf16[192,1024]{1,0:T(8,128)(2,1)} fusion(bf16[192,4096]{1,0:T(8,128)(2,1)} %all_heads.1, bf16[4096,1024]{1,0:T(8,128)(2,1)} %param.23, f32[192]{0:T(256)S(1)} %add_sqrt_fusion), kind=kOutput, calls=%fused_computation.2 | convolution fusion | flops 1611005952 | bytes 10355456 | tf_op jit(solution)/shard_map/dot_general | solution.py:762
  102.7 0.0 copy-done
  102.7 0.6 convert_element_type.19.cv
  103.3 34.5 %delta_rule.1 = bf16[192,1024]{1,0:T(8,128)(2,1)} custom-call(bf16[192,1024]{1,0:T(8,128)(2,1)} %fusion.value_in, f32[4,1024]{1,0:T(4,128)} %convert_element_type.19.cv, bf16[8,192,192]{2,1,0:T(8,128)(2,1)} %get-tuple-element.14.h_in, bf16[8,192,128]{2,1,0:T(8,128)(2,1)} %get-tuple-element.15.eff_in, bf16[8,128,192]{2,1,0:T(8,128)(2,1)} %get-tuple-element.16.g_in, ...), custom_call_target="tpu_custom_call" | custom-call | tf_op jit(solution)/shard_map/delta_rule/pallas_call | solution.py:679
  137.8 1.8 %copy.20 = bf16[192,1024]{1,0:T(8,128)(2,1)} copy(bf16[192,1024]{1,0:T(8,128)(2,1)} %delta_rule.1) | data formatting | bytes 786432
  (2 shorter events, 0.0 us)
Async XLA Ops:
  96.3 6.4 %copy-start = (bf16[4,1024]{1,0:T(4,128)(2,1)S(1)}, bf16[4,1024]{1,0:T(4,128)(2,1)}, u32[]{:S(2)}) copy-start(bf16[4,1024]{1,0:T(4,128)(2,1)} %param.28) | copy-start | bytes 24580
where the time goes:
time: 140 us
  Pallas kernels  120 us (86%)
  other arithmetic  9.01 us (6%)
  matrix products  6.42 us (5%)
  local copies, waits for them, and re-layouts  4.39 us (3%)
    pallas_call x1, Pallas kernels, linear(): pl.pallas_call(linear_kernel, out_shape=(jax.ShapeDtypeStruct((HEADS, ROW...  53.9 us
    pallas_call x1, Pallas kernels, delta(): pl.pallas_call(delta_kernel, out_shape=jax.ShapeDtypeStruct((ROWS, 1024),...  34.5 us
    pallas_call x1, Pallas kernels, attention(): pl.pallas_call(attention_kernel, out_shape=jax.ShapeDtypeStruct((ROWS, 10...  17 us
    pallas_call x1, Pallas kernels, all_heads(): pl.pallas_call(heads_kernel, out_shape=jax.ShapeDtypeStruct((ROWS, 4096),...  14.4 us
    dot_general x1, matrix products, body(): summed = jnp.dot(everything, value_proj, preferred_element_type=F32)  6.42 us

commit v1 on v0

--- a/solution.py
+++ b/solution.py
@@ -319,14 +319,43 @@
     )(slots, kv, segs, seg_query, queries, gate)
 
 
+def mm(a, b, precision=None):
+    return jnp.dot(a, b, precision=precision, preferred_element_type=F32)
+
+
+def mm_t(a, b, precision=None):
+    return lax.dot_general(
+        a, b, (((1,), (1,)), ((), ())), precision=precision, preferred_element_type=F32
+    )
+
+
+def split(x):
+    high = x.astype(BF16)
+    return high, (x - high.astype(F32)).astype(BF16)
+
+
+def mm_split(a, b, product=mm):
+    (ah, al), (bh, bl) = a, b
+    return product(ah, bh) + (product(ah, bl) + product(al, bh))
+
+
+def mm_low(a, b):
+    return mm(a.astype(BF16), b.astype(BF16))
+
+
 PIECES = 3
 
 
-def heads_kernel(own, out, l_sem, p_s, p_r, a_s, a_r, f_s, f_r):
+def heads_kernel(
+    own, t_own, out, px_out, mz_out, t_all, row_sc, p_own, p_all,
+    l_sem, p_s, p_r, a_s, a_r, f_s, f_r, ts, tr, zs, zr,
+):
     ctx, head, z, place, y_hi, x, y_lo, core = coords()
     partner = (ctx, y_lo * 2 + 1 - core)
     across = (ctx, (1 - y_lo) * 2 + core)
-    greet([partner, across])
+    plane = [(z * 8 + lax.rem(place + d, 8), head) for d in range(1, 8)]
+    column = [(lax.rem(z + d, 8) * 8 + place, head) for d in range(1, 8)]
+    greet([partner, across] + plane + column)
     size = ROWS // PIECES
 
     def part(i, h):
@@ -336,61 +365,97 @@
         return own.at[pl.ds(i * size, size)]
 
     far, farther = (1 - y_lo) * 2 + core, (1 - y_lo) * 2 + 1 - core
+    sends = []
+    for d in range(1, 8):
+        owner = lax.rem(place + d, 8)
+        copy = push(t_own.at[owner], t_all.at[8 - d], ts.at[d - 1], tr.at[7 - d], plane[d - 1])
+        copy.start()
+        sends.append(copy)
     keep = [pltpu.make_async_copy(piece(i), part(i, head), l_sem.at[i]) for i in range(PIECES)]
     for i in range(PIECES):
         push(piece(i), part(i, head), a_s.at[i], a_r.at[i], across).start()
         push(piece(i), part(i, head), p_s.at[i], p_r.at[i], partner).start()
         keep[i].start()
-    for i in range(PIECES):
+
+    def pass_on(i):
         push(piece(i), part(i, far), a_s.at[i], a_r.at[i], across).wait_recv()
         push(part(i, far), part(i, far), f_s.at[i], f_r.at[i], partner).start()
+
+    unit_k = jnp.where(
+        lax.broadcasted_iota(jnp.int32, (128, 128), 0)
+        == lax.broadcasted_iota(jnp.int32, (128, 128), 1),
+        1.0,
+        0.0,
+    )
+    t_all[0] = t_own[place]
+    row_sc[...] = jnp.zeros(row_sc.shape, F32)
+    row_sc[:, 0:128] = unit_k
+    px_out[0] = row_sc[...].astype(BF16)
+    for d in range(1, 8):
+        push(t_own.at[0], t_all.at[8 - d], ts.at[d - 1], tr.at[7 - d], plane[d - 1]).wait_recv()
+    pass_on(0)
+    for i in range(8):
+        current = t_all[lax.rem(i - place + 8, 8)]
+        width = (i + 1) * 128
+        high, low = split(row_sc[:, 0:width])
+        row_sc[:, 0:width] = mm(current, high) + mm(current, low)
+        row_sc[:, width : width + 128] = unit_k
+        px_out[i + 1] = row_sc[...].astype(BF16)
+        if i == 4:
+            pass_on(1)
+    p_own[...] = row_sc[:, 0:128].astype(BF16)
+    for d in range(1, 8):
+        copy = push(p_own, p_all.at[d - 1], zs.at[d - 1], zr.at[d - 1], column[d - 1])
+        copy.start()
+        sends.append(copy)
+    pass_on(2)
+    for d in range(1, 8):
+        push(p_own, p_all.at[d - 1], zs.at[d - 1], zr.at[d - 1], column[d - 1]).wait_recv()
+    running = unit_k
+    for r in range(1, 8):
+        valid = z >= r
+        mz_out[:, (r - 1) * 128 : r * 128] = jnp.where(valid, running, 0.0).astype(BF16)
+        if r < 7:
+            high, low = split(running)
+            running = mm(high, p_all[r - 1]) + mm(low, p_all[r - 1])
     for i in range(PIECES):
         near = y_lo * 2 + 1 - core
         push(piece(i), part(i, near), p_s.at[i], p_r.at[i], partner).wait()
         push(part(i, far), part(i, farther), f_s.at[i], f_r.at[i], partner).wait()
         push(piece(i), part(i, far), a_s.at[i], a_r.at[i], across).wait_send()
         keep[i].wait()
-
-
-def all_heads(own):
+    for copy in sends:
+        copy.wait_send()
+
+
+def all_heads(own, transitions):
     dma = pltpu.SemaphoreType.DMA
+    vmem = pl.BlockSpec(memory_space=pltpu.VMEM)
     return pl.pallas_call(
         heads_kernel,
-        out_shape=jax.ShapeDtypeStruct((ROWS, 4096), BF16),
-        in_specs=[pl.BlockSpec(memory_space=pltpu.VMEM)],
-        out_specs=pl.BlockSpec(memory_space=pl.ANY),
-        scratch_shapes=[dma((PIECES,))] * 7,
+        out_shape=(
+            jax.ShapeDtypeStruct((ROWS, 4096), BF16),
+            jax.ShapeDtypeStruct((9, 128, 1152), BF16),
+            jax.ShapeDtypeStruct((128, 896), BF16),
+        ),
+        in_specs=[vmem] * 2,
+        out_specs=[pl.BlockSpec(memory_space=pl.ANY), vmem, vmem],
+        scratch_shapes=[
+            pltpu.VMEM((8, 128, 128), BF16),
+            pltpu.VMEM((128, 1152), F32),
+            pltpu.VMEM((128, 128), BF16),
+            pltpu.VMEM((7, 128, 128), BF16),
+        ]
+        + [dma((PIECES,))] * 7
+        + [dma((7,))] * 4,
         compiler_params=pltpu.CompilerParams(collective_id=1, has_side_effects=True),
         name="all_heads",
-    )(own)
-
-
-def mm(a, b, precision=None):
-    return jnp.dot(a, b, precision=precision, preferred_element_type=F32)
-
-
-def mm_t(a, b, precision=None):
-    return lax.dot_general(
-        a, b, (((1,), (1,)), ((), ())), precision=precision, preferred_element_type=F32
-    )
-
-
-def split(x):
-    high = x.astype(BF16)
-    return high, (x - high.astype(F32)).astype(BF16)
-
-
-def mm_split(a, b, product=mm):
-    (ah, al), (bh, bl) = a, b
-    return product(ah, bh) + (product(ah, bl) + product(al, bh))
-
-
-def mm_low(a, b):
-    return mm(a.astype(BF16), b.astype(BF16))
+    )(own, transitions)
 
 
 def causal(ext, taps, width):
     total = jnp.zeros((ROWS, width), F32)
+    taps = taps[...].astype(F32)
     for m in range(4):
         total = total + taps[m : m + 1, :] * ext[13 + m : 13 + m + ROWS, 0:width]
     return total / (1.0 + jnp.exp(-total))
@@ -435,23 +500,20 @@
 
 
 def linear_kernel(
-    lq, lk, cq, ck, decay, beta, keys, values, seg,
-    h_out, eff_out, g_out, px_out, mz_out, kv, segs,
+    lq, lk, cq, ck, decay_logits, beta_logits, decay_base, decay_bias, keys, values, seg,
+    h_out, eff_out, g_out, t_own, kv, segs,
     own, own_seg, w_load, wy_s, wy_r, wz_s, wz_r, wx_s, wx_r, wf_s, wf_r,
-    halo, ext, q_sc, k_sc, t_own, t_all, row_sc, p_own, p_all,
-    hs, hr, ts, tr, zs, zr,
+    halo, ext, q_sc, k_sc, row_sc, hs, hr,
 ):
     ctx, head, z, place, y_hi, x, y_lo, core = coords()
     following = (lax.rem(ctx + 1, 64), head)
     previous = (lax.rem(ctx + 63, 64), head)
-    plane = [(z * 8 + lax.rem(place + d, 8), head) for d in range(1, 8)]
-    column = [(lax.rem(z + d, 8) * 8 + place, head) for d in range(1, 8)]
     transfers = window_steps(
         keys, values, seg, kv, segs, own, own_seg, w_load,
         wy_s, wy_r, wz_s, wz_r, wx_s, wx_r, wf_s, wf_r,
     )
     next(transfers)
-    greet([previous] + plane + column + window_sources())
+    greet([previous] + window_sources())
     tail = pl.ds(ROWS - 16, 16)
     edge = [
         push(lq.at[tail], halo.at[0], hs.at[0], hr.at[0], following),
@@ -486,9 +548,19 @@
         1.0,
         0.0,
     )
-    sum_row = mm_t(decay[...], ones, HIGH)
-    sum_col = mm_t(ones, decay[...], HIGH)
-    beta_col = mm_t(unit, beta[...], HIGH)
+    shifted = decay_logits[...] + decay_bias[...]
+    softplus = jnp.maximum(shifted, 0.0) + jnp.log1p(jnp.exp(-jnp.abs(shifted)))
+    decay = -jnp.exp(decay_base[...]) * softplus
+    beta_col = jax.nn.sigmoid(beta_logits[...])
+    onward = jnp.where(row <= col, 1.0, 0.0)
+    sum_col = mm(ones, decay, HIGH)
+    across_rows = (((0,), (0,)), ((), ()))
+    row_sc[0] = lax.dot_general(
+        decay, onward, across_rows, precision=HIGH, preferred_element_type=F32
+    )
+    row_sc[1] = lax.dot_general(
+        beta_col, unit, across_rows, precision=HIGH, preferred_element_type=F32
+    )
     group = 2
     for base in range(0, HEADS, group):
         parts, systems = [], []
@@ -498,8 +570,8 @@
                 k_split = split(k)
                 key_key = mm_split(k_split, k_split, mm_t)
                 query_key = mm_split(split(q), k_split, mm_t)
-            c_col, c_row = sum_col[:, e : e + 1], sum_row[e : e + 1, :]
-            b_col, b_row = beta_col[:, e : e + 1], beta[e : e + 1, :]
+            c_col, c_row = sum_col[:, e : e + 1], row_sc[0, e : e + 1, :]
+            b_col, b_row = beta_col[:, e : e + 1], row_sc[1, e : e + 1, :]
             fade = jnp.exp(jnp.where(lower, c_col - c_row, NEGATIVE))
             systems.append(jnp.where(strict, b_col * key_key * fade, 0.0))
             parts.append((q, k, c_col, b_col, b_row, query_key * fade))
@@ -519,47 +591,11 @@
             t_own[e] = (jnp.exp(final) * unit_k - mm_split(decayed, weight_keys)).astype(BF16)
             g_out[e] = (mm_split(decayed, inverse) * b_row).astype(BF16)
         next(transfers, None)
-
-    sends = []
-    for d in range(1, 8):
-        owner = lax.rem(place + d, 8)
-        copy = push(t_own.at[owner], t_all.at[8 - d], ts.at[d - 1], tr.at[7 - d], plane[d - 1])
-        copy.start()
-        sends.append(copy)
-    t_all[0] = t_own[place]
-    for d in range(1, 8):
-        push(t_own.at[0], t_all.at[8 - d], ts.at[d - 1], tr.at[7 - d], plane[d - 1]).wait_recv()
-    row_sc[...] = jnp.zeros(row_sc.shape, F32)
-    row_sc[:, 0:128] = unit_k
-    px_out[0] = row_sc[...].astype(BF16)
-    for i in range(8):
-        current = t_all[lax.rem(i - place + 8, 8)]
-        width = (i + 1) * 128
-        high, low = split(row_sc[:, 0:width])
-        row_sc[:, 0:width] = mm(current, high) + mm(current, low)
-        row_sc[:, width : width + 128] = unit_k
-        px_out[i + 1] = row_sc[...].astype(BF16)
-    p_own[...] = row_sc[:, 0:128].astype(BF16)
-    for d in range(1, 8):
-        copy = push(p_own, p_all.at[d - 1], zs.at[d - 1], zr.at[d - 1], column[d - 1])
-        copy.start()
-        sends.append(copy)
-    for d in range(1, 8):
-        push(p_own, p_all.at[d - 1], zs.at[d - 1], zr.at[d - 1], column[d - 1]).wait_recv()
-    running = unit_k
-    for r in range(1, 8):
-        valid = z >= r
-        mz_out[:, (r - 1) * 128 : r * 128] = jnp.where(valid, running, 0.0).astype(BF16)
-        if r < 7:
-            high, low = split(running)
-            running = mm(high, p_all[r - 1]) + mm(low, p_all[r - 1])
-    for copy in sends:
-        copy.wait_send()
     for _ in transfers:
         pass
 
 
-def linear(lq, lk, cq, ck, decay, beta, keys, values, seg_tile):
+def linear(*operands):
     dma = pltpu.SemaphoreType.DMA
     vmem = pl.BlockSpec(memory_space=pltpu.VMEM)
     anywhere = pl.BlockSpec(memory_space=pl.ANY)
@@ -569,13 +605,12 @@
             jax.ShapeDtypeStruct((HEADS, ROWS, ROWS), BF16),
             jax.ShapeDtypeStruct((HEADS, ROWS, 128), BF16),
             jax.ShapeDtypeStruct((HEADS, 128, ROWS), BF16),
-            jax.ShapeDtypeStruct((9, 128, 1152), BF16),
-            jax.ShapeDtypeStruct((128, 896), BF16),
+            jax.ShapeDtypeStruct((HEADS, 128, 128), BF16),
             jax.ShapeDtypeStruct((3, 2, 4, ROWS, 512), BF16),
             jax.ShapeDtypeStruct((4, 3, 2, 8, 128), jnp.int32),
         ),
-        in_specs=[vmem] * 6 + [anywhere] * 3,
-        out_specs=[vmem] * 5 + [anywhere] * 2,
+        in_specs=[vmem] * 8 + [anywhere] * 3,
+        out_specs=[vmem] * 4 + [anywhere] * 2,
         scratch_shapes=[
             pltpu.VMEM((2, ROWS, 512), BF16),
             pltpu.VMEM((8, 128), jnp.int32),
@@ -592,26 +627,18 @@
             pltpu.VMEM((16 + ROWS, 512), F32),
             pltpu.VMEM((4, ROWS, 128), F32),
             pltpu.VMEM((4, ROWS, 128), F32),
-            pltpu.VMEM((8, 128, 128), BF16),
-            pltpu.VMEM((8, 128, 128), BF16),
-            pltpu.VMEM((128, 1152), F32),
-            pltpu.VMEM((128, 128), BF16),
-            pltpu.VMEM((7, 128, 128), BF16),
+            pltpu.VMEM((2, HEADS, ROWS), F32),
             dma((2,)),
             dma((2,)),
-            dma((7,)),
-            dma((7,)),
-            dma((7,)),
-            dma((7,)),
         ],
         compiler_params=pltpu.CompilerParams(collective_id=2, has_side_effects=True),
         name="linear_operators",
-    )(lq, lk, cq, ck, decay, beta, keys, values, seg_tile)
+    )(*operands)
 
 
 def delta_kernel(
     value_in, cv, h_in, eff_in, g_in, px_in, mz_in, attn, gate, gain, rezero, out,
-    halo, ext, v_sc, b_own, b_all, local, l_own, l_all, within, s_own, s_all,
+    halo, ext, v_sc, b_own, b_all, local, gated_sc, l_own, l_all, within, s_own, s_all,
     hs, hr, bs, br, zs, zr, ss, sr,
 ):
     ctx, head, z, place, y_hi, x, y_lo, core = coords()
@@ -648,6 +675,10 @@
         sends.append(copy)
     for i in range(8):
         within[i] = mm(px_in[i, :, 128:1152], blocks)
+    for e in range(HEADS):
+        cols = slice(e * 128, (e + 1) * 128)
+        g = gate[:, cols].astype(F32)
+        gated_sc[e] = rezero[:, cols] * gain[...] * (g * jax.nn.sigmoid(g))
     for d in range(1, 8):
         push(l_own, l_all.at[d - 1], zs.at[d - 1], zr.at[d - 1], column[d - 1]).wait_recv()
     entry = mm(mz_in[...], l_all[...].reshape(7 * 128, 128)).astype(BF16)
@@ -666,9 +697,7 @@
         cols = slice(e * 128, (e + 1) * 128)
         delta = local[e] + mm(eff_in[e], s_all[e])
         norm = delta / jnp.sqrt(jnp.mean(delta * delta, axis=1, keepdims=True) + EPSILON)
-        g = gate[:, cols].astype(F32)
-        gated = norm * gain[...] * (g * jax.nn.sigmoid(g))
-        out[:, cols] = (attn[:, cols].astype(F32) + rezero[:, cols] * gated).astype(BF16)
+        out[:, cols] = (attn[:, cols].astype(F32) + norm * gated_sc[e]).astype(BF16)
     for copy in sends:
         copy.wait_send()
 
@@ -687,6 +716,7 @@
             pltpu.VMEM((ROWS, 1024), BF16),
             pltpu.VMEM((8, 128, 128), BF16),
             pltpu.VMEM((8, 128, 128), BF16),
+            pltpu.VMEM((8, ROWS, 128), F32),
             pltpu.VMEM((8, ROWS, 128), F32),
             pltpu.VMEM((128, 128), BF16),
             pltpu.VMEM((7, 128, 128), BF16),
@@ -729,17 +759,15 @@
 ):
     ctx = lax.axis_index("ctx")
     seg_tile = jnp.pad(segment_ids, (0, 1024 - ROWS), constant_values=127).reshape(8, 128)
-    log_decay = -jnp.exp(decay_base)[:, None] * jax.nn.softplus(
-        decay_logits.T + decay_bias[:, None]
-    )
-    beta = jax.nn.sigmoid(beta_logits.T)
-    *ops, kv, segs = linear(
+    *ops, transitions, kv, segs = linear(
         linear_queries,
         linear_keys,
-        conv_queries.astype(F32),
-        conv_keys.astype(F32),
-        log_decay,
-        beta,
+        conv_queries,
+        conv_keys,
+        decay_logits,
+        beta_logits,
+        decay_base.reshape(1, HEADS),
+        decay_bias.reshape(1, HEADS),
         attention_keys,
         attention_values,
         seg_tile,
@@ -757,14 +785,14 @@
     attn_out = attention(
         slots, kv.reshape(24, ROWS, 512), segs.reshape(24, 8, 128), seg_query, queries, attn_gate
     )
-    everything = all_heads(attn_out)
+    everything, px, mz = all_heads(attn_out, transitions)
     squares = jnp.mean(jnp.square(everything.astype(F32)), axis=1, keepdims=True)
     summed = jnp.dot(everything, value_proj, preferred_element_type=F32)
     value_in = (summed / jnp.sqrt(squares + EPSILON)).astype(BF16)
     return delta(
         value_in,
-        conv_values.astype(F32),
-        ops,
+        conv_values,
+        (*ops, px, mz),
         attn_out,
         output_gate,
         output_gain.reshape(1, 128),

time: 140 us -> 136 us (0.971)
  other arithmetic: 9.01 us -> 2.45 us
  local copies, waits for them, and re-layouts: 4.39 us -> 7.29 us
    pallas_call x1, Pallas kernels: 53.9 us -> 40.3 us  [linear(): pl.pallas_call(linear_kernel, out_shape=(jax.ShapeDtypeStruct((HEADS, ROW...]
    pallas_call x1, Pallas kernels: 14.4 us -> 27.6 us  [all_heads(): pl.pallas_call(heads_kernel, out_shape=(jax.ShapeDtypeStruct((ROWS, 4096)...]
    convert_element_type x3 -> x0, other arithmetic: 3.17 us -> none  [the longest x1 1.29 us: body(): conv_queries.astype(F32)]
    unnamed x3, local copies, waits for them, and re-layouts: 1.77 us -> 4.67 us
where the time goes in v1:
time: 136 us; the launch traced here: 135 us
  Pallas kernels  119 us (88%)
  local copies, waits for them, and re-layouts  7.29 us (5%)
  matrix products  6.41 us (5%)
  other arithmetic  2.45 us (2%)
    pallas_call x1, Pallas kernels, linear(): pl.pallas_call(linear_kernel, out_shape=(jax.ShapeDtypeStruct((HEADS, ROW...  40.3 us
    pallas_call x1, Pallas kernels, delta(): pl.pallas_call(delta_kernel, out_shape=jax.ShapeDtypeStruct((ROWS, 1024),...  33.9 us
    pallas_call x1, Pallas kernels, all_heads(): pl.pallas_call(heads_kernel, out_shape=(jax.ShapeDtypeStruct((ROWS, 4096)...  27.6 us
    pallas_call x1, Pallas kernels, attention(): pl.pallas_call(attention_kernel, out_shape=jax.ShapeDtypeStruct((ROWS, 10...  17 us
    dot_general x1, matrix products, body(): summed = jnp.dot(everything, value_proj, preferred_element_type=F32)  6.41 us
    unnamed x3, local copies, waits for them, and re-layouts  4.67 us

profile of v1, /device:TPU:8, one launch (start us, length us, event | category | flops | bytes accessed | tf_op | source)
XLA Modules:
  0.0 135.0 jit_solution(5329370742325488004)
XLA Ops:
  0.0 0.6 pad_add_fusion.slots
  0.6 0.7 tile.2
  1.3 0.7 reshape_tile.3.seg_query
  2.0 1.3 pad_bitcast_fusion.seg
  3.3 1.5 %copy.19.decay_logits = f32[192,8]{1,0:T(8,128)} copy(f32[192,8]{0,1:T(8,128)} %param.29) | data formatting | bytes 12288 | tf_op args[11]
  4.7 1.5 %copy.20.beta_logits = f32[192,8]{1,0:T(8,128)} copy(f32[192,8]{0,1:T(8,128)} %param.30) | data formatting | bytes 12288 | tf_op args[12]
  6.2 40.3 %linear_operators.1 = (bf16[8,192,192]{2,1,0:T(8,128)(2,1)}, bf16[8,192,128]{2,1,0:T(8,128)(2,1)}, bf16[8,128,192]{2,1,0:T(8,128)(2,1)}, bf16[8,128,128]{2,1,0:T...) custom-call(bf16[192,512]{1,0:T(8,128)(2,1)} %lq.1, bf16[192,512]{1,0:T(8,128)(2,1)} %lk.1, ...), custom_call_target="tpu_custom_call" | custom-call | tf_op jit(solution)/shard_map/linear_operators/pallas_call | solution.py:602
  46.4 17.0 %window_attention.1.own.attn = bf16[192,1024]{1,0:T(8,128)(2,1)} custom-call(s32[35]{0:T(128)} %pad_add_fusion.slots, bf16[24,192,512]{2,1,0:T(8,128)(2,1)} %bitcast.11, s32[24,8,128]{2,1,0:T(8,128)} %bitcast.12, s32[1,768]{1,0:T(1,128)} %reshape_tile.3.seg_query, bf16[192,1024]{1,0:T(8,128)(2,1)} %queries.1, bf16[192,1024]{1,0:T(8,128)(2,1)} %gate.2), custom_call_target="tpu_custom_call" | custom-call | tf_op jit(solution)/shard_map/window_attention/pallas_call | solution.py:293
  63.5 27.6 %all_heads.1 = (bf16[192,4096]{1,0:T(8,128)(2,1)}, bf16[9,128,1152]{2,1,0:T(8,128)(2,1)}, bf16[128,896]{1,0:T(8,128)(2,1)}) custom-call(bf16[192,1024]{1,0:T(8,128)(2,1)} %window_attention.1.own.attn, bf16[8,128,128]{2,1,0:T(8,128)(2,1)} %get-tuple-element.16.t_own), custom_call_target="tpu_custom_call" | custom-call | tf_op jit(solution)/shard_map/all_heads/pallas_call | solution.py:434
  91.1 1.8 %multiply_reduce_fusion = f32[192]{0:T(256)S(1)} fusion(bf16[192,4096]{1,0:T(8,128)(2,1)} %get-tuple-element.17), kind=kLoop, calls=%fused_computation | loop fusion | flops 2359104 | bytes 1573632 | tf_op jit(solution)/shard_map/reduce_sum | solution.py:789
  92.9 6.4 %fusion.value_in = bf16[192,1024]{1,0:T(8,128)(2,1)} fusion(bf16[192,4096]{1,0:T(8,128)(2,1)} %get-tuple-element.17, bf16[4096,1024]{1,0:T(8,128)(2,1)} %param.23, f32[192]{0:T(256)S(1)} %add_sqrt_fusion), kind=kOutput, calls=%fused_computation.2 | convolution fusion | flops 1611005952 | bytes 10355456 | tf_op jit(solution)/shard_map/dot_general | solution.py:790
  99.3 33.9 %delta_rule.1 = bf16[192,1024]{1,0:T(8,128)(2,1)} custom-call(bf16[192,1024]{1,0:T(8,128)(2,1)} %fusion.value_in, bf16[4,1024]{1,0:T(4,128)(2,1)} %cv.1, bf16[8,192,192]{2,1,0:T(8,128)(2,1)} %get-tuple-element.18.h_in, bf16[8,192,128]{2,1,0:T(8,128)(2,1)} %get-tuple-element.19.eff_in, bf16[8,128,192]{2,1,0:T(8,128)(2,1)} %get-tuple-element.20.g_in, ...), custom_call_target="tpu_custom_call" | custom-call | tf_op jit(solution)/shard_map/delta_rule/pallas_call | solution.py:708
  133.2 1.8 %copy.22 = bf16[192,1024]{1,0:T(8,128)(2,1)} copy(bf16[192,1024]{1,0:T(8,128)(2,1)} %delta_rule.1) | data formatting | bytes 786432
  (2 shorter events, 0.0 us)

commit v2 on v1

--- a/solution.py
+++ b/solution.py
@@ -347,7 +347,7 @@
 
 
 def heads_kernel(
-    own, t_own, out, px_out, mz_out, t_all, row_sc, p_own, p_all,
+    own, t_own, out, px_out, sx_out, t_out, mz_out, t_all, p_own, p_all,
     l_sem, p_s, p_r, a_s, a_r, f_s, f_r, ts, tr, zs, zr,
 ):
     ctx, head, z, place, y_hi, x, y_lo, core = coords()
@@ -388,22 +388,24 @@
         0.0,
     )
     t_all[0] = t_own[place]
-    row_sc[...] = jnp.zeros(row_sc.shape, F32)
-    row_sc[:, 0:128] = unit_k
-    px_out[0] = row_sc[...].astype(BF16)
     for d in range(1, 8):
         push(t_own.at[0], t_all.at[8 - d], ts.at[d - 1], tr.at[7 - d], plane[d - 1]).wait_recv()
     pass_on(0)
     for i in range(8):
-        current = t_all[lax.rem(i - place + 8, 8)]
-        width = (i + 1) * 128
-        high, low = split(row_sc[:, 0:width])
-        row_sc[:, 0:width] = mm(current, high) + mm(current, low)
-        row_sc[:, width : width + 128] = unit_k
-        px_out[i + 1] = row_sc[...].astype(BF16)
+        t_out[i] = t_all[lax.rem(i - place + 8, 8)]
+    before, after = unit_k, unit_k
+    for i in range(8):
+        px_out[i] = before.astype(BF16)
+        high, low = split(before)
+        before = mm(t_out[i], high) + mm(t_out[i], low)
+        j = 7 - i
+        sx_out[:, j * 128 : (j + 1) * 128] = after.astype(BF16)
+        if j > 0:
+            high, low = split(after)
+            after = mm(high, t_out[j]) + mm(low, t_out[j])
         if i == 4:
             pass_on(1)
-    p_own[...] = row_sc[:, 0:128].astype(BF16)
+    p_own[...] = before.astype(BF16)
     for d in range(1, 8):
         copy = push(p_own, p_all.at[d - 1], zs.at[d - 1], zr.at[d - 1], column[d - 1])
         copy.start()
@@ -435,14 +437,15 @@
         heads_kernel,
         out_shape=(
             jax.ShapeDtypeStruct((ROWS, 4096), BF16),
-            jax.ShapeDtypeStruct((9, 128, 1152), BF16),
+            jax.ShapeDtypeStruct((8, 128, 128), BF16),
+            jax.ShapeDtypeStruct((128, 1024), BF16),
+            jax.ShapeDtypeStruct((8, 128, 128), BF16),
             jax.ShapeDtypeStruct((128, 896), BF16),
         ),
         in_specs=[vmem] * 2,
-        out_specs=[pl.BlockSpec(memory_space=pl.ANY), vmem, vmem],
+        out_specs=[pl.BlockSpec(memory_space=pl.ANY)] + [vmem] * 4,
         scratch_shapes=[
             pltpu.VMEM((8, 128, 128), BF16),
-            pltpu.VMEM((128, 1152), F32),
             pltpu.VMEM((128, 128), BF16),
             pltpu.VMEM((7, 128, 128), BF16),
         ]
@@ -548,19 +551,19 @@
         1.0,
         0.0,
     )
-    shifted = decay_logits[...] + decay_bias[...]
+    same = lax.broadcasted_iota(jnp.int32, (HEADS, HEADS), 0) == lax.broadcasted_iota(
+        jnp.int32, (HEADS, HEADS), 1
+    )
+    base = jnp.sum(jnp.where(same, decay_base[...], 0.0), axis=1, keepdims=True)
+    bias = jnp.sum(jnp.where(same, decay_bias[...], 0.0), axis=1, keepdims=True)
+    shifted = decay_logits[...] + bias
     softplus = jnp.maximum(shifted, 0.0) + jnp.log1p(jnp.exp(-jnp.abs(shifted)))
-    decay = -jnp.exp(decay_base[...]) * softplus
-    beta_col = jax.nn.sigmoid(beta_logits[...])
-    onward = jnp.where(row <= col, 1.0, 0.0)
-    sum_col = mm(ones, decay, HIGH)
-    across_rows = (((0,), (0,)), ((), ()))
-    row_sc[0] = lax.dot_general(
-        decay, onward, across_rows, precision=HIGH, preferred_element_type=F32
-    )
-    row_sc[1] = lax.dot_general(
-        beta_col, unit, across_rows, precision=HIGH, preferred_element_type=F32
-    )
+    decay = -jnp.exp(base) * softplus
+    beta = jax.nn.sigmoid(beta_logits[...])
+    row_sc[0] = mm_t(decay, ones, HIGH)
+    row_sc[1] = beta
+    sum_col = mm_t(ones, decay, HIGH)
+    beta_col = mm_t(unit, beta, HIGH)
     group = 2
     for base in range(0, HEADS, group):
         parts, systems = [], []
@@ -637,7 +640,7 @@
 
 
 def delta_kernel(
-    value_in, cv, h_in, eff_in, g_in, px_in, mz_in, attn, gate, gain, rezero, out,
+    value_in, cv, h_in, eff_in, g_in, px_in, sx_in, t_in, mz_in, attn, gate, gain, rezero, out,
     halo, ext, v_sc, b_own, b_all, local, gated_sc, l_own, l_all, within, s_own, s_all,
     hs, hr, bs, br, zs, zr, ss, sr,
 ):
@@ -668,13 +671,18 @@
         source = lax.rem(place + 8 - d, 8)
         push(b_own.at[0], b_all.at[source], bs.at[d - 1], br.at[d - 1], plane[d - 1]).wait_recv()
     blocks = b_all[...].reshape(8 * 128, 128)
-    l_own[...] = mm(px_in[8, :, 128:1152], blocks).astype(BF16)
+    l_own[...] = mm(sx_in[...], blocks).astype(BF16)
     for d in range(1, 8):
         copy = push(l_own, l_all.at[d - 1], zs.at[d - 1], zr.at[d - 1], column[d - 1])
         copy.start()
         sends.append(copy)
-    for i in range(8):
-        within[i] = mm(px_in[i, :, 128:1152], blocks)
+    within[0] = jnp.zeros((128, 128), F32)
+    running = b_all[0].astype(F32)
+    within[1] = running
+    for i in range(1, 7):
+        high, low = split(running)
+        running = mm(t_in[i], high) + mm(t_in[i], low) + b_all[i].astype(F32)
+        within[i + 1] = running
     for e in range(HEADS):
         cols = slice(e * 128, (e + 1) * 128)
         g = gate[:, cols].astype(F32)
@@ -683,7 +691,7 @@
         push(l_own, l_all.at[d - 1], zs.at[d - 1], zr.at[d - 1], column[d - 1]).wait_recv()
     entry = mm(mz_in[...], l_all[...].reshape(7 * 128, 128)).astype(BF16)
     for i in range(8):
-        s_own[i] = (mm(px_in[i, :, 0:128], entry) + within[i]).astype(BF16)
+        s_own[i] = (mm(px_in[i], entry) + within[i]).astype(BF16)
     for d in range(1, 8):
         target = lax.rem(place + d, 8)
         copy = push(s_own.at[target], s_all.at[place], ss.at[d - 1], sr.at[d - 1], plane[d - 1])
@@ -708,7 +716,7 @@
     return pl.pallas_call(
         delta_kernel,
         out_shape=jax.ShapeDtypeStruct((ROWS, 1024), BF16),
-        in_specs=[vmem] * 11,
+        in_specs=[vmem] * 13,
         out_specs=vmem,
         scratch_shapes=[
             pltpu.VMEM((16, 1024), BF16),
@@ -764,8 +772,8 @@
         linear_keys,
         conv_queries,
         conv_keys,
-        decay_logits,
-        beta_logits,
+        decay_logits.T,
+        beta_logits.T,
         decay_base.reshape(1, HEADS),
         decay_bias.reshape(1, HEADS),
         attention_keys,
@@ -781,18 +789,18 @@
     slots = jnp.concatenate(
         [step * 8 + y_hi * 4 + x, x * 6 + step * 2 + y_hi, missing]
     ).astype(jnp.int32)
-    seg_query = jnp.tile(segment_ids, 4).reshape(1, 4 * ROWS)
+    seg_query = jnp.concatenate([segment_ids.reshape(1, ROWS)] * 4, axis=1)
     attn_out = attention(
         slots, kv.reshape(24, ROWS, 512), segs.reshape(24, 8, 128), seg_query, queries, attn_gate
     )
-    everything, px, mz = all_heads(attn_out, transitions)
+    everything, *scan = all_heads(attn_out, transitions)
     squares = jnp.mean(jnp.square(everything.astype(F32)), axis=1, keepdims=True)
     summed = jnp.dot(everything, value_proj, preferred_element_type=F32)
     value_in = (summed / jnp.sqrt(squares + EPSILON)).astype(BF16)
     return delta(
         value_in,
         conv_values,
-        (*ops, px, mz),
+        (*ops, *scan),
         attn_out,
         output_gate,
         output_gain.reshape(1, 128),

time: 136 us -> 131 us (0.963)
  local copies, waits for them, and re-layouts: 7.29 us -> 3.04 us
  Pallas kernels: 119 us -> 117 us
  other arithmetic: 2.45 us -> 3.99 us
    unnamed x3 -> x1, local copies, waits for them, and re-layouts: 4.67 us -> 1.77 us
    concatenate x0 -> x1, other arithmetic: none -> 1.48 us  [body(): seg_query = jnp.concatenate([segment_ids.reshape(1, ROWS)] * 4, axis=1)]
where the time goes in v2:
time: 131 us
  Pallas kernels  117 us (89%)
  matrix products  6.41 us (5%)
  other arithmetic  3.99 us (3%)
  local copies, waits for them, and re-layouts  3.04 us (2%)
    pallas_call x1, Pallas kernels, linear(): pl.pallas_call(linear_kernel, out_shape=(jax.ShapeDtypeStruct((HEADS, ROW...  40.3 us
    pallas_call x1, Pallas kernels, delta(): pl.pallas_call(delta_kernel, out_shape=jax.ShapeDtypeStruct((ROWS, 1024),...  33.4 us
    pallas_call x1, Pallas kernels, all_heads(): pl.pallas_call(heads_kernel, out_shape=(jax.ShapeDtypeStruct((ROWS, 4096)...  26.6 us
    pallas_call x1, Pallas kernels, attention(): pl.pallas_call(attention_kernel, out_shape=jax.ShapeDtypeStruct((ROWS, 10...  17 us
    dot_general x1, matrix products, body(): summed = jnp.dot(everything, value_proj, preferred_element_type=F32)  6.41 us

profile of v2, /device:TPU:8, one launch (start us, length us, event | category | flops | bytes accessed | tf_op | source)
XLA Modules:
  0.0 130.7 jit_solution(7621173637687785622)
XLA Ops:
  0.0 0.7 pad_add_fusion.1.slots
  0.7 1.5 %pad_add_fusion.seg_query = s32[1,768]{1,0:T(1,128)} fusion(s32[1,192]{1,0:T(1,128)} %bitcast.18), kind=kLoop, calls=%fused_computation.4 | loop fusion | flops 2304 | bytes 3840 | tf_op jit(solution)/shard_map/concatenate | solution.py:792
  2.2 1.3 pad_bitcast_fusion.seg
  3.5 40.3 %linear_operators.1 = (bf16[8,192,192]{2,1,0:T(8,128)(2,1)}, bf16[8,192,128]{2,1,0:T(8,128)(2,1)}, bf16[8,128,192]{2,1,0:T(8,128)(2,1)}, bf16[8,128,128]{2,1,0:T...) custom-call(bf16[192,512]{1,0:T(8,128)(2,1)} %lq.1, bf16[192,512]{1,0:T(8,128)(2,1)} %lk.1, ...), custom_call_target="tpu_custom_call" | custom-call | tf_op jit(solution)/shard_map/linear_operators/pallas_call | solution.py:605
  43.8 17.0 %window_attention.1.own.attn = bf16[192,1024]{1,0:T(8,128)(2,1)} custom-call(s32[35]{0:T(128)} %pad_add_fusion.1.slots, bf16[24,192,512]{2,1,0:T(8,128)(2,1)} %bitcast.14, s32[24,8,128]{2,1,0:T(8,128)} %bitcast.15, s32[1,768]{1,0:T(1,128)} %pad_add_fusion.seg_query, bf16[192,1024]{1,0:T(8,128)(2,1)} %queries.1, bf16[192,1024]{1,0:T(8,128)(2,1)} %gate.2), custom_call_target="tpu_custom_call" | custom-call | tf_op jit(solution)/shard_map/window_attention/pallas_call | solution.py:293
  60.8 26.6 %all_heads.1 = (bf16[192,4096]{1,0:T(8,128)(2,1)}, bf16[8,128,128]{2,1,0:T(8,128)(2,1)}, bf16[128,1024]{1,0:T(8,128)(2,1)}, bf16[8,128,128]{2,1,0:T(8,128)(2,1)}, bf16[128,896]{1,0:T(8,128)(2,1)}) custom-call(bf16[192,1024]{1,0:T(8,128)(2,1)} %window_attention.1.own.attn, bf16[8,128,128]{2,1,0:T(8,128)(2,1)} %get-tuple-element.18.t_own), custom_call_target="tpu_custom_call" | custom-call | tf_op jit(solution)/shard_map/all_heads/pallas_call | solution.py:436
  87.3 1.8 %multiply_reduce_fusion = f32[192]{0:T(256)S(1)} fusion(bf16[192,4096]{1,0:T(8,128)(2,1)} %get-tuple-element.19), kind=kLoop, calls=%fused_computation | loop fusion | flops 2359104 | bytes 1573632 | tf_op jit(solution)/shard_map/reduce_sum | solution.py:797
  89.1 6.4 %fusion.value_in = bf16[192,1024]{1,0:T(8,128)(2,1)} fusion(bf16[192,4096]{1,0:T(8,128)(2,1)} %get-tuple-element.19, bf16[4096,1024]{1,0:T(8,128)(2,1)} %param.23, f32[192]{0:T(256)S(1)} %add_sqrt_fusion), kind=kOutput, calls=%fused_computation.2 | convolution fusion | flops 1611005952 | bytes 10355456 | tf_op jit(solution)/shard_map/dot_general | solution.py:798
  95.6 33.4 %delta_rule.1 = bf16[192,1024]{1,0:T(8,128)(2,1)} custom-call(bf16[192,1024]{1,0:T(8,128)(2,1)} %fusion.value_in, bf16[4,1024]{1,0:T(4,128)(2,1)} %cv.1, bf16[8,192,192]{2,1,0:T(8,128)(2,1)} %get-tuple-element.20.h_in, bf16[8,192,128]{2,1,0:T(8,128)(2,1)} %get-tuple-element.21.eff_in, bf16[8,128,192]{2,1,0:T(8,128)(2,1)} %get-tuple-element.22.g_in, ...), custom_call_target="tpu_custom_call" | custom-call | tf_op jit(solution)/shard_map/delta_rule/pallas_call | solution.py:716
  129.0 1.8 %copy.20 = bf16[192,1024]{1,0:T(8,128)(2,1)} copy(bf16[192,1024]{1,0:T(8,128)(2,1)} %delta_rule.1) | data formatting | bytes 786432
  (2 shorter events, 0.0 us)
